TPU v7x, 32 devices: a whole 2x2x4 slice. The times are simulated.
32 devices in a mesh: dp: 8 (over y, x, core), mp: 4 (over z).
Axes of the slice: x: 2, y: 2, z: 4, core: 2. Of those that a mesh axis runs over, the one named last changes fastest.
Arguments:
- patches: bfloat16 [1024, 6144], P('dp', 'mp'), may hold values from -64 to 64
- send_start: int32 [8, 8], P('dp'), may hold values from 0 to 128, as said below
- run_length: int32 [8, 8], P('dp'), may hold values from 0 to 32, as said below
- slot_start: int32 [8, 8], P('dp'), may hold values from 0 to 128, as said below
- image_ids: int32 [8, 128], P('dp'), may hold values from 0 to 7, never falling along the last dimension, each value on 1 to 32 neighbouring positions
- norm_gain: float32 [6144], replicated, may hold values from 0.1 to 1.9
- qkv_weight: bfloat16 [6144, 3, 4096], P('dp', None, 'mp'), may hold values from -0.078125 to 0.078125
- query_gain: float32 [128], replicated, may hold values from 0.1 to 1.9
- key_gain: float32 [128], replicated, may hold values from 0.1 to 1.9
- out_weight: bfloat16 [4096, 6144], P('mp'), may hold values from -0.09375 to 0.09375
Outputs:
- packed: bfloat16 [1024, 6144], P('dp', 'mp')
- attended: bfloat16 [1024, 6144], P('dp', 'mp')
Inputs may be any that keep to these rules, and one draw needn't show every extreme that they name: `run_length`: every source's runs sum to 128 and every pack's runs sum to 128; the longest run is exactly 32. `send_start`: the runs of one source device do not intersect and cover its 128 rows. `slot_start`: the runs into one pack do not intersect and fill its 128 slots. `image_ids`: image numbers never fall along a pack; equal numbers mark one image.
All inputs are finite; a program needn't handle non-finite values.
Results may differ from a plain program's by a relative error of at most 0.011.
Values may be sent and summed in bfloat16 or wider, within the bound.
A program may use at most 128 MiB of HBM per device.

v0:
```python
import jax
import jax.numpy as jnp
from jax import lax
from jax.sharding import PartitionSpec as P

epsilon = 1e-06


def row_norm(values, scales):
    middle = jnp.mean(values, axis=-1, keepdims=True)
    spread = jnp.mean(values * values, axis=-1, keepdims=True) - middle * middle
    return (values - middle) * lax.rsqrt(spread + epsilon) * scales


def on_device(
    patches,
    send_start,
    run_length,
    slot_start,
    image_ids,
    norm_gain,
    qkv_weight,
    query_gain,
    key_gain,
    out_weight,
):
    pack_rows, feat_local = patches.shape
    pack_count = lax.axis_size("dp")
    capacity = 2 * pack_rows // pack_count
    local_cols = qkv_weight.shape[1] * qkv_weight.shape[2]
    offsets = jnp.arange(capacity, dtype=jnp.int32)
    source_rows = jnp.clip(send_start[0][:, None] + offsets[None, :], 0, pack_rows - 1)
    occupied = offsets[None, :] < run_length[0][:, None]
    outgoing = jnp.where(occupied[:, :, None], patches[source_rows], jnp.zeros((), jnp.bfloat16))
    arrived = lax.all_to_all(outgoing, "dp", split_axis=0, concat_axis=0, tiled=True)
    targets = (slot_start[0][:, None] + offsets[None, :]).reshape(-1)
    packed = (
        jnp.zeros((pack_rows, feat_local), jnp.bfloat16)
        .at[targets]
        .add(arrived.reshape(-1, feat_local), mode="drop")
    )
    full_rows = lax.all_gather(packed, "mp", axis=1, tiled=True).astype(jnp.float32)
    normed = row_norm(full_rows, norm_gain).astype(jnp.bfloat16)
    portion = lax.all_gather(qkv_weight, "dp", axis=0, tiled=True)
    projected = jnp.dot(
        normed, portion.reshape(portion.shape[0], local_cols), preferred_element_type=jnp.float32
    )
    head_size = query_gain.shape[0]
    heads_here = qkv_weight.shape[2] // head_size
    split_heads = projected.reshape(pack_rows, 3, heads_here, head_size)
    queries = row_norm(split_heads[:, 0], query_gain).astype(jnp.bfloat16)
    key_rows = row_norm(split_heads[:, 1], key_gain).astype(jnp.bfloat16)
    values = split_heads[:, 2].astype(jnp.bfloat16)
    scores = jnp.einsum(
        "qhd,khd->hqk", queries, key_rows, preferred_element_type=jnp.float32
    ) * head_size ** (-0.5)
    image_of = image_ids[0]
    same_image = image_of[:, None] == image_of[None, :]
    weights_raw = jnp.where(same_image[None], jnp.exp(scores), 0.0)
    totals = jnp.sum(weights_raw, axis=-1, keepdims=True)
    attention = (weights_raw / totals).astype(jnp.bfloat16)
    context = jnp.einsum(
        "hqk,khd->qhd", attention, values, preferred_element_type=jnp.float32
    ).astype(jnp.bfloat16)
    context = context.reshape(pack_rows, heads_here * head_size)
    partial_value = jnp.dot(context, out_weight, preferred_element_type=jnp.float32)
    attended = lax.psum_scatter(
        partial_value.astype(jnp.bfloat16), "mp", scatter_dimension=1, tiled=True
    )
    return (packed, attended)


def solution(mesh):
    return jax.shard_map(
        on_device,
        mesh=mesh,
        in_specs=(
            P("dp", "mp"),
            P("dp", None),
            P("dp", None),
            P("dp", None),
            P("dp", None),
            P(),
            P("dp", None, "mp"),
            P(),
            P(),
            P("mp", None),
        ),
        out_specs=(P("dp", "mp"), P("dp", "mp")),
        check_vma=False,
    )
```

profile of v0, /device:TPU:0, one launch (start us, length us, event | category | flops | bytes accessed | tf_op | source)
XLA Modules:
  0.0 316.1 jit_solution(7269659442975579226)
XLA Ops:
  7.2 0.8 compare_select_fusion
  8.0 0.1 reshape.210
  8.0 0.7 iota_compare_fusion
  8.8 1.3 gather_fusion
  10.1 1.0 broadcast_select_fusion
  11.1 5.2 %all-to-all-start = ((bf16[8,32,1536]{2,1,0:T(8,128)(2,1)}), bf16[8,32,1536]{2,1,0:T(8,128)(2,1)S(1)}, u32[]{:S(2)}, u32[]{:S(2)}) async-start(bf16[8,32,1536]{2,1,0:T(8,128)(2,1)} %broadcast_select_fusion), calls=%async_computation | async-start | bytes 1572864 | tf_op jit(solution)/shard_map/all_to_all | solution.py:35
  16.3 0.1 iota_add_fusion
  16.4 0.1 add.111
  16.4 12.4 %all-to-all-done = bf16[8,32,1536]{2,1,0:T(8,128)(2,1)S(1)} async-done(((bf16[8,32,1536]{2,1,0:T(8,128)(2,1)}), bf16[8,32,1536]{2,1,0:T(8,128)(2,1)S(1)}, u32[]{:S(2)}, u32[]{:S(2)}) %all-to-all-start) | async-done | bytes 786464 | tf_op jit(solution)/shard_map/all_to_all | solution.py:35
  28.8 3.9 %scatter_custom_fusion = bf16[128,1536]{1,0:T(8,128)(2,1)} fusion(s32[256]{0:T(256)S(1)} %bitcast.58, bf16[256,1536]{1,0:T(8,128)(2,1)S(1)} %bitcast.55, bf16[]{:T(256)} %constant.9.clone.1), kind=kCustom, calls=%fused_computation.44 | custom fusion | flops 393216 | bytes 393218 | tf_op jit(solution)/shard_map/scatter-add | solution.py:40
  32.8 0.0 all-gather.5.cloned.1.call-start
  32.8 6.7 %copy.15 = bf16[768,3,1024]{0,2,1:T(8,128)(2,1)} copy(bf16[768,3,1024]{2,0,1:T(8,128)(2,1)} %param.16) | data formatting | bytes 9437184 | tf_op args[6]
  39.6 0.6 copy-done.3
  40.1 0.1 broadcast_compare_fusion
  40.2 29.2 %all-gather.3.cloned.1.call-done = bf16[128,6144]{1,0:T(8,128)(2,1)} async-done(((bf16[128,1536]{1,0:T(8,128)(2,1)}), bf16[128,6144]{1,0:T(8,128)(2,1)}) %all-gather.3.cloned.1.call-update) | async-done | bytes 1572880 | tf_op jit(solution)/shard_map/all_gather | solution.py:42
  69.4 1.9 convert_reduce_fusion
  71.3 177.6 %all-gather.5.cloned.1.call-done = bf16[6144,3,1024]{0,2,1:T(8,128)(2,1)} async-done(((bf16[768,3,1024]{0,2,1:T(8,128)(2,1)}), bf16[6144,3,1024]{0,2,1:T(8,128)(2,1)}) %all-gather.5.cloned.1.call-update) | async-done | bytes 37748752 | tf_op jit(solution)/shard_map/all_gather | solution.py:44
  249.0 16.6 %fusion.5 = f32[128,3,8,128]{0,3,2,1:T(8,128)S(1)} fusion(bf16[3,8,128,6144]{3,2,1,0:T(8,128)(2,1)} %bitcast.53, bf16[128,6144]{1,0:T(8,128)(2,1)} %all-gather.3.cloned.1.call-done, f32[6144]{0:T(1024)S(1)} %copy-done.2, f32[128]{0:T(128)S(1)} %get-tuple-element.13, f32[128]{0:T(128)S(1)} %get-tuple-element.12), kind=kOutput, calls=%fused_computation.11 | convolution fusion | flops 4835770368 | bytes 40920064 | tf_op jit(solution)/shard_map/dot_general | solution.py:45
  265.6 0.1 slice_reduce_fusion.1
  265.7 0.1 fusion.19
  265.8 0.4 fusion.11
  266.2 0.2 convolution_convert_fusion.1
  266.5 7.7 %convolution_convert_fusion = bf16[128,6144]{1,0:T(8,128)(2,1)} fusion(bf16[128,1024]{0,1:T(8,128)(2,1)S(1)} %bitcast.56, bf16[1024,6144]{1,0:T(8,128)(2,1)} %param.19), kind=kOutput, calls=%fused_computation.2 | convolution fusion | flops 1611399168 | bytes 14417920 | tf_op jit(solution)/shard_map/dot_general | solution.py:66
  274.2 35.4 %reduce-scatter.2.cloned.1.call-done = bf16[128,1536]{1,0:T(8,128)(2,1)} async-done(((bf16[128,6144]{1,0:T(8,128)(2,1)}), bf16[128,1536]{1,0:T(8,128)(2,1)}) %reduce-scatter.2.cloned.1.call-update) | async-done | bytes 393232 | tf_op jit(solution)/shard_map/reduce_scatter | solution.py:67
  (22 shorter events, 0.2 us)
Async XLA Ops:
  7.2 1.6 copy-start
  10.0 6.2 %copy-start.4 = (s32[1,8]{1,0:T(1,128)S(1)}, s32[1,8]{1,0:T(1,128)}, u32[]{:S(2)}) copy-start(s32[1,8]{1,0:T(1,128)} %param.13) | copy-start | bytes 100
  11.1 17.8 %all-to-all-start = ((bf16[8,32,1536]{2,1,0:T(8,128)(2,1)}), bf16[8,32,1536]{2,1,0:T(8,128)(2,1)S(1)}, u32[]{:S(2)}, u32[]{:S(2)}) async-start(bf16[8,32,1536]{2,1,0:T(8,128)(2,1)} %broadcast_select_fusion), calls=%async_computation | async-start | bytes 1572864 | tf_op jit(solution)/shard_map/all_to_all | solution.py:35
  16.2 53.2 %all-gather.3.cloned.1.call-start = ((), (), s32[]{:S(2)}) async-start(), calls=%async_computation.2 | async-start | bytes 1966080 | tf_op jit(solution)/shard_map/all_gather | solution.py:42
  32.8 216.2 %all-gather.5.cloned.1.call-start = ((), (), s32[]{:S(2)}) async-start(), calls=%async_computation.3 | async-start | bytes 42467328 | tf_op jit(solution)/shard_map/all_gather | solution.py:44
  39.5 0.7 copy-start.3
  39.5 209.5 %copy-start.2 = (f32[6144]{0:T(1024)S(1)}, f32[6144]{0:T(1024)}, u32[]{:S(2)}) copy-start(f32[6144]{0:T(1024)} %param.15) | copy-start | bytes 73732
  39.5 270.1 %reduce-scatter.2.cloned.1.call-start = ((), (), s32[]{:S(2)}) async-start(), calls=%async_computation.4 | async-start | bytes 1966080 | tf_op jit(solution)/shard_map/reduce_scatter | solution.py:67
  249.0 16.9 %copy-start.5 = (f32[128]{0:T(128)S(1)}, f32[128]{0:T(128)}, u32[]{:S(2)}) copy-start(f32[128]{0:T(128)} %param.18) | copy-start | bytes 1540
  249.0 16.9 %copy-start.6 = (f32[128]{0:T(128)S(1)}, f32[128]{0:T(128)}, u32[]{:S(2)}) copy-start(f32[128]{0:T(128)} %param.17) | copy-start | bytes 1540
  266.5 43.1 %copy-start.1 = (bf16[128,1536]{1,0:T(8,128)(2,1)S(1)}, bf16[128,1536]{1,0:T(8,128)(2,1)}, u32[]{:S(2)}) copy-start(bf16[128,1536]{1,0:T(8,128)(2,1)} %param.10) | copy-start | bytes 1179652
Sparse Core Ops, SparseCore 0:
  32.9 36.4 all-gather.2
  71.3 177.5 all-gather.4
  274.3 35.2 reduce-scatter.1
where the time goes:
time: 317 us; the launch traced here: 316 us
  waiting for transfers between devices  255 us (80%)
  matrix products  24.9 us (8%)
  between operations  13.9 us (4%)
  local copies, waits for them, and re-layouts  8.7 us (3%)
  other arithmetic  8.67 us (3%)
  starting transfers between devices  5.29 us (2%)
    all_gather x1, waiting for transfers between devices, on_device(): portion = lax.all_gather(qkv_weight, 'dp', axis=0, tiled=True)  178 us
    reduce_scatter x1, waiting for transfers between devices, on_device(): lax.psum_scatter(partial_value.astype(jnp.bfloat16), 'mp', scatter_dimens...  35.4 us
    all_gather x1, waiting for transfers between devices, on_device(): lax.all_gather(packed, 'mp', axis=1, tiled=True).astype(jnp.float32)  29.2 us
    dot_general x1, matrix products, on_device(): jnp.dot(normed, portion.reshape(portion.shape[0], local_cols), preferred_...  16.6 us
    all_to_all x1, waiting for transfers between devices, on_device(): lax.all_to_all(outgoing, 'dp', split_axis=0, concat_axis=0, tiled=True)  12.4 us
    dot_general x1, matrix products, on_device(): jnp.dot(context, out_weight, preferred_element_type=jnp.float32)  7.65 us
    unnamed x15, local copies, waits for them, and re-layouts  7.28 us
  transfers between devices with their start and end apart: 4, of which 4 were waited for; matrix products, arithmetic and copies ran while one was open for 3% of the time, Pallas kernels for 0%

commit v1 on v0

--- a/solution.py
+++ b/solution.py
@@ -26,25 +26,52 @@
 ):
     pack_rows, feat_local = patches.shape
     pack_count = lax.axis_size("dp")
+    mp_count = lax.axis_size("mp")
     capacity = 2 * pack_rows // pack_count
     local_cols = qkv_weight.shape[1] * qkv_weight.shape[2]
     offsets = jnp.arange(capacity, dtype=jnp.int32)
-    source_rows = jnp.clip(send_start[0][:, None] + offsets[None, :], 0, pack_rows - 1)
+    rows = jnp.arange(pack_rows, dtype=jnp.int32)
+
+    x = patches.astype(jnp.float32)
+    sums = jnp.stack([jnp.sum(x, axis=-1), jnp.sum(x * x, axis=-1)])
+    sums = lax.psum(sums, "mp") / (feat_local * mp_count)
+    middle = sums[0][:, None]
+    spread = sums[1][:, None] - middle * middle
+    gain = lax.dynamic_slice_in_dim(norm_gain, lax.axis_index("mp") * feat_local, feat_local)
+    normed = ((x - middle) * lax.rsqrt(spread + epsilon) * gain).astype(jnp.bfloat16)
+
+    wide = lax.all_gather(normed, "mp", axis=1, tiled=True)
+    slices = lax.all_to_all(wide, "dp", split_axis=1, concat_axis=0, tiled=True)
+
+    tables = jnp.concatenate([send_start, run_length, slot_start], axis=0)[None]
+    tables = lax.all_gather(tables, "dp", axis=0, tiled=True)
+    starts, lengths, slots = tables[:, 0].T, tables[:, 1].T, tables[:, 2]
+    inside = (rows >= slots[:, :, None]) & (rows < (slots + lengths)[:, :, None])
+    base = jnp.arange(pack_count, dtype=jnp.int32)[None, :] * pack_rows + starts - slots
+    origin = jnp.sum(jnp.where(inside, base[:, :, None] + rows, 0), axis=1).reshape(-1)
+    chosen = (origin[:, None] == jnp.arange(origin.shape[0], dtype=jnp.int32)).astype(jnp.bfloat16)
+    ordered = jnp.dot(chosen, slices, preferred_element_type=jnp.float32).astype(jnp.bfloat16)
+
+    partial = jnp.dot(
+        ordered, qkv_weight.reshape(qkv_weight.shape[0], local_cols), preferred_element_type=jnp.float32
+    ).astype(jnp.bfloat16)
+    projected = lax.psum_scatter(partial, "dp", scatter_dimension=0, tiled=True).astype(jnp.float32)
+
+    own_rows = send_start[0][:, None] + offsets[None, :]
     occupied = offsets[None, :] < run_length[0][:, None]
-    outgoing = jnp.where(occupied[:, :, None], patches[source_rows], jnp.zeros((), jnp.bfloat16))
-    arrived = lax.all_to_all(outgoing, "dp", split_axis=0, concat_axis=0, tiled=True)
+    pick = (occupied[:, :, None] & (own_rows[:, :, None] == rows)).astype(jnp.bfloat16)
+    outgoing = jnp.dot(
+        pick.reshape(-1, pack_rows), patches, preferred_element_type=jnp.float32
+    ).astype(jnp.bfloat16)
+    arrived = lax.all_to_all(
+        outgoing.reshape(pack_count, capacity, feat_local), "dp", split_axis=0, concat_axis=0, tiled=True
+    )
     targets = (slot_start[0][:, None] + offsets[None, :]).reshape(-1)
-    packed = (
-        jnp.zeros((pack_rows, feat_local), jnp.bfloat16)
-        .at[targets]
-        .add(arrived.reshape(-1, feat_local), mode="drop")
-    )
-    full_rows = lax.all_gather(packed, "mp", axis=1, tiled=True).astype(jnp.float32)
-    normed = row_norm(full_rows, norm_gain).astype(jnp.bfloat16)
-    portion = lax.all_gather(qkv_weight, "dp", axis=0, tiled=True)
-    projected = jnp.dot(
-        normed, portion.reshape(portion.shape[0], local_cols), preferred_element_type=jnp.float32
-    )
+    place = (rows[:, None] == targets[None, :]).astype(jnp.bfloat16)
+    packed = jnp.dot(
+        place, arrived.reshape(-1, feat_local), preferred_element_type=jnp.float32
+    ).astype(jnp.bfloat16)
+
     head_size = query_gain.shape[0]
     heads_here = qkv_weight.shape[2] // head_size
     split_heads = projected.reshape(pack_rows, 3, heads_here, head_size)

time: 317 us -> 221 us (0.70)
  waiting for transfers between devices: 255 us -> 123 us
  blocking collectives: 0 us -> 37.5 us
  other arithmetic: 8.67 us -> 2.56 us
  local copies, waits for them, and re-layouts: 8.7 us -> 12.6 us
    all_gather x2 -> x1, waiting for transfers between devices: 207 us -> 35.5 us  [on_device(): wide = lax.all_gather(normed, 'mp', axis=1, tiled=True)]
    reduce_scatter x0 -> x1, waiting for transfers between devices: none -> 59.1 us  [on_device(): lax.psum_scatter(partial, 'dp', scatter_dimension=0, tiled=True)]
    all_gather x0 -> x1, blocking collectives: none -> 24 us  [on_device(): tables = lax.all_gather(tables, 'dp', axis=0, tiled=True)]
    reduce_scatter x1, waiting for transfers between devices: 35.4 us -> 16 us  [on_device(): lax.psum_scatter(partial_value.astype(jnp.bfloat16), 'mp', scatter_dimens...]
    psum x0 -> x1, blocking collectives: none -> 13.5 us  [on_device(): sums = lax.psum(sums, 'mp') / (feat_local * mp_count)]
    scatter-add x1 -> x0, other arithmetic: 3.91 us -> none  [on_device(): packed = jnp.zeros((pack_rows, feat_local), jnp.bfloat16).at[targets].add...]
    unnamed x15 -> x18, local copies, waits for them, and re-layouts: 7.28 us -> 10.7 us
    all_to_all x1 -> x2, starting transfers between devices: 5.17 us -> 7.33 us  [the longest x1 3.79 us: on_device(): slices = lax.all_to_all(wide, 'dp', split_axis=1, concat_axis=0, tiled=True)]
  transfers between devices with their start and end apart: 4 -> 5, of which waited for: 4 -> 4; matrix products, arithmetic and copies ran while one was open for 3% -> 4% of each run, Pallas kernels for 0% -> 0%
where the time goes in v1:
time: 221 us; the launch traced here: 220 us
  waiting for transfers between devices  123 us (56%)
  blocking collectives  37.5 us (17%)
  matrix products  23.2 us (10%)
  between operations  13.9 us (6%)
  local copies, waits for them, and re-layouts  12.6 us (6%)
  starting transfers between devices  7.45 us (3%)
  other arithmetic  2.56 us (1%)
    reduce_scatter x1, waiting for transfers between devices, on_device(): lax.psum_scatter(partial, 'dp', scatter_dimension=0, tiled=True)  59.1 us
    all_gather x1, waiting for transfers between devices, on_device(): wide = lax.all_gather(normed, 'mp', axis=1, tiled=True)  35.5 us
    all_gather x1, blocking collectives, on_device(): tables = lax.all_gather(tables, 'dp', axis=0, tiled=True)  24 us
    reduce_scatter x1, waiting for transfers between devices, on_device(): lax.psum_scatter(partial_value.astype(jnp.bfloat16), 'mp', scatter_dimens...  16 us
    psum x1, blocking collectives, on_device(): sums = lax.psum(sums, 'mp') / (feat_local * mp_count)  13.5 us
    all_to_all x1, waiting for transfers between devices, on_device(): lax.all_to_all(outgoing.reshape(pack_count, capacity, feat_local), 'dp',...  12.4 us
    dot_general x1, matrix products, on_device(): jnp.dot(ordered, qkv_weight.reshape(qkv_weight.shape[0], local_cols), pre...  12.2 us
    unnamed x18, local copies, waits for them, and re-layouts  10.7 us
  transfers between devices with their start and end apart: 5, of which 4 were waited for; matrix products, arithmetic and copies ran while one was open for 4% of the time, Pallas kernels for 0%

profile of v1, /device:TPU:0, one launch (start us, length us, event | category | flops | bytes accessed | tf_op | source)
XLA Modules:
  0.0 220.3 jit_solution(4133471638652877734)
XLA Ops:
  7.2 1.2 copy.47
  8.7 13.5 %psum.7 = f32[2,128]{1,0:T(2,128)S(1)} all-reduce(f32[2,128]{1,0:T(2,128)S(1)} %pad_maximum_fusion), channel_id=1, replica_groups=mesh['dp'=8,'mp'=4] {'mp'}, use_global_device_ids=true, to_apply=%region_3.4 | all-reduce | flops 256 | bytes 2048 | tf_op jit(solution)/shard_map/psum | solution.py:37
  22.1 0.8 dynamic_slice.3
  22.9 1.0 fusion.8
  24.0 35.5 %all-gather.4.cloned.1.call-done = bf16[128,6144]{0,1:T(8,128)(2,1)} async-done(((bf16[128,1536]{0,1:T(8,128)(2,1)}), bf16[128,6144]{0,1:T(8,128)(2,1)}) %all-gather.4.cloned.1.call-update) | async-done | bytes 1572880 | tf_op jit(solution)/shard_map/all_gather | solution.py:43
  59.4 3.8 %all-to-all-start.1 = ((bf16[128,8,768]{0,2,1:T(8,128)(2,1)}), bf16[128,8,768]{0,2,1:T(8,128)(2,1)S(1)}, u32[]{:S(2)}, u32[]{:S(2)}) async-start(bf16[128,8,768]{0,2,1:T(8,128)(2,1)} %bitcast.83), calls=%async_computation.1 | async-start | bytes 3145728 | tf_op jit(solution)/shard_map/all_to_all | solution.py:44
  63.3 24.0 %all-gather.1 = s32[8,3,8]{2,1,0:T(4,128)S(1)} all-gather(s32[1,3,8]{2,1,0:T(4,128)S(1)} %add_bitcast_fusion), channel_id=2, replica_groups=mesh['dp'=8,'mp'=4] {'dp'}, dimensions={0}, use_global_device_ids=true | all-gather | bytes 864 | tf_op jit(solution)/shard_map/all_gather | solution.py:47
  87.5 6.7 %copy.49 = bf16[768,3,1024]{0,2,1:T(8,128)(2,1)} copy(bf16[768,3,1024]{2,0,1:T(8,128)(2,1)} %param.16) | data formatting | bytes 9437184 | tf_op args[6]
  94.3 0.7 copy.48
  95.0 12.2 %convolution_convert_fusion.1 = bf16[1024,3072]{1,0:T(8,128)(2,1)} fusion(bf16[768,3072]{0,1:T(8,128)(2,1)} %bitcast.79, bf16[1024,768]{1,0:T(8,128)(2,1)S(1)} %bitcast.84, s32[1024]{0:T(1024)S(1)} %bitcast.91), kind=kOutput, calls=%fused_computation.1 | convolution fusion | flops 6447431680 | bytes 12587008 | tf_op jit(solution)/shard_map/dot_general | solution.py:55
  107.4 0.6 copy-done.1
  108.0 59.1 %reduce-scatter.3.cloned.1.call-done = bf16[128,3072]{1,0:T(8,128)(2,1)} async-done(((bf16[1024,3072]{1,0:T(8,128)(2,1)}), bf16[128,3072]{1,0:T(8,128)(2,1)}) %reduce-scatter.3.cloned.1.call-update) | async-done | bytes 786448 | tf_op jit(solution)/shard_map/reduce_scatter | solution.py:58
  167.2 1.3 copy.58
  168.7 0.3 slice_reduce_fusion.1
  169.0 0.3 fusion.16
  169.7 0.7 fusion.4
  170.4 0.3 convolution_convert_fusion.4
  170.7 7.6 %convolution_convert_fusion = bf16[128,6144]{1,0:T(8,128)(2,1)} fusion(bf16[128,1024]{0,1:T(8,128)(2,1)S(1)} %bitcast.86, bf16[1024,6144]{1,0:T(8,128)(2,1)} %param.19), kind=kOutput, calls=%fused_computation | convolution fusion | flops 1611399168 | bytes 14417920 | tf_op jit(solution)/shard_map/dot_general | solution.py:93
  178.6 0.7 copy-done
  179.3 1.3 convolution_convert_fusion.2
  180.6 3.5 %all-to-all-start = ((bf16[8,32,1536]{2,1,0:T(8,128)(2,1)}), bf16[8,32,1536]{2,1,0:T(8,128)(2,1)S(1)}, u32[]{:S(2)}, u32[]{:S(2)}) async-start(bf16[8,32,1536]{2,1,0:T(8,128)(2,1)} %bitcast.3), calls=%async_computation | async-start | bytes 1572864 | tf_op jit(solution)/shard_map/all_to_all | solution.py:66
  184.3 12.4 %all-to-all-done = bf16[8,32,1536]{2,1,0:T(8,128)(2,1)S(1)} async-done(((bf16[8,32,1536]{2,1,0:T(8,128)(2,1)}), bf16[8,32,1536]{2,1,0:T(8,128)(2,1)S(1)}, u32[]{:S(2)}, u32[]{:S(2)}) %all-to-all-start) | async-done | bytes 786464 | tf_op jit(solution)/shard_map/all_to_all | solution.py:66
  196.7 1.0 convolution_convert_fusion.3
  197.7 16.0 %reduce-scatter.5.cloned.1.call-done = bf16[128,1536]{1,0:T(8,128)(2,1)} async-done(((bf16[128,6144]{1,0:T(8,128)(2,1)}), bf16[128,1536]{1,0:T(8,128)(2,1)}) %reduce-scatter.5.cloned.1.call-update) | async-done | bytes 393232 | tf_op jit(solution)/shard_map/reduce_scatter | solution.py:94
  (42 shorter events, 1.7 us)
Async XLA Ops:
  7.2 52.3 %all-gather.4.cloned.1.call-start = ((), (), s32[]{:S(2)}) async-start(), calls=%async_computation.4 | async-start | bytes 1966080 | tf_op jit(solution)/shard_map/all_gather | solution.py:43
  59.4 3.8 %copy-start.2 = (s32[1,8]{1,0:T(1,128)S(1)}, s32[1,8]{1,0:T(1,128)}, u32[]{:S(2)}) copy-start(s32[1,8]{1,0:T(1,128)} %param.11) | copy-start | bytes 100
  59.4 3.8 %copy-start.3 = (s32[1,8]{1,0:T(1,128)S(1)}, s32[1,8]{1,0:T(1,128)}, u32[]{:S(2)}) copy-start(s32[1,8]{1,0:T(1,128)} %param.13) | copy-start | bytes 100
  59.4 3.9 %copy-start.4 = (s32[1,8]{1,0:T(1,128)S(1)}, s32[1,8]{1,0:T(1,128)}, u32[]{:S(2)}) copy-start(s32[1,8]{1,0:T(1,128)} %param.12) | copy-start | bytes 100
  59.4 34.9 %all-to-all-start.1 = ((bf16[128,8,768]{0,2,1:T(8,128)(2,1)}), bf16[128,8,768]{0,2,1:T(8,128)(2,1)S(1)}, u32[]{:S(2)}, u32[]{:S(2)}) async-start(bf16[128,8,768]{0,2,1:T(8,128)(2,1)} %bitcast.83), calls=%async_computation.1 | async-start | bytes 3145728 | tf_op jit(solution)/shard_map/all_to_all | solution.py:44
  63.2 103.9 %reduce-scatter.3.cloned.1.call-start = ((), (), s32[]{:S(2)}) async-start(), calls=%async_computation.5 | async-start | bytes 7077888 | tf_op jit(solution)/shard_map/reduce_scatter | solution.py:58
  107.3 0.7 copy-start.1
  107.3 106.4 %reduce-scatter.5.cloned.1.call-start = ((), (), s32[]{:S(2)}) async-start(), calls=%async_computation.6 | async-start | bytes 1966080 | tf_op jit(solution)/shard_map/reduce_scatter | solution.py:94
  168.6 1.0 copy-start.5
  168.7 1.0 copy-start.6
  178.3 1.0 copy-start
  180.6 16.1 %all-to-all-start = ((bf16[8,32,1536]{2,1,0:T(8,128)(2,1)}), bf16[8,32,1536]{2,1,0:T(8,128)(2,1)S(1)}, u32[]{:S(2)}, u32[]{:S(2)}) async-start(bf16[8,32,1536]{2,1,0:T(8,128)(2,1)} %bitcast.3), calls=%async_computation | async-start | bytes 1572864 | tf_op jit(solution)/shard_map/all_to_all | solution.py:66
Sparse Core Ops, SparseCore 0:
  24.1 35.2 all-gather.3
  107.4 59.6 reduce-scatter.2
  178.4 35.2 reduce-scatter.4

commit v2 on v1

--- a/solution.py
+++ b/solution.py
@@ -1,6 +1,10 @@
+import functools
+
 import jax
 import jax.numpy as jnp
 from jax import lax
+from jax.experimental import pallas as pl
+from jax.experimental.pallas import tpu as pltpu
 from jax.sharding import PartitionSpec as P
 
 epsilon = 1e-06
@@ -12,7 +16,7 @@
     return (values - middle) * lax.rsqrt(spread + epsilon) * scales
 
 
-def on_device(
+def plain_on_device(
     patches,
     send_start,
     run_length,
@@ -97,9 +101,336 @@
     return (packed, attended)
 
 
+MESH = pl.DeviceIdType.MESH
+BF = jnp.bfloat16
+F32 = jnp.float32
+
+
+def fused_kernel(
+    x_ref, ss_ref, rl_ref, sl_ref, ids_ref, ng_ref, qg_ref, kg_ref, w_hbm, ow_hbm,
+    packed_ref, out_ref,
+    w_ref, ow_ref, zbuf, nbuf, gbuf, outr, arr, tscr, tabs, perm, ordr,
+    sbuf, rbuf, cbuf, crecv, qn, kn, vn, ctx, pbuf, zrecv,
+    w_sem, zs, zr, asem, ar, rs, rr, ts, tr, ssem, sr, cs, cr, ps, pr,
+):
+    rows, feat = x_ref.shape
+    n_dp, cap = outr.shape[0], outr.shape[1]
+    kdim, cols = w_ref.shape[1], w_ref.shape[2]
+    half = n_dp // 2 * rows
+    d = lax.axis_index("dp")
+    z = lax.axis_index("mp")
+    k = d % 2
+    cx = (d // 2) % 2
+    cy = d // 4
+
+    def peer_chip(oc):
+        return ((cy + oc // 2) % 2) * 2 + (cx + oc % 2) % 2
+
+    def peer(o):
+        return peer_chip(o // 2) * 2 + (k + o % 2) % 2
+
+    def remote(src, dst, s, r, dd, zz):
+        return pltpu.make_async_remote_copy(
+            src_ref=src, dst_ref=dst, send_sem=s, recv_sem=r,
+            device_id=(dd, zz), device_id_type=MESH,
+        )
+
+    w_copy = pltpu.make_async_copy(w_hbm, w_ref, w_sem.at[0])
+    ow_copy = pltpu.make_async_copy(ow_hbm, ow_ref, w_sem.at[1])
+    w_copy.start()
+    ow_copy.start()
+
+    tscr[...] = jnp.zeros_like(tscr)
+    tscr[0:1, 0:n_dp] = ss_ref[...]
+    tscr[1:2, 0:n_dp] = rl_ref[...]
+    tscr[2:3, 0:n_dp] = sl_ref[...]
+
+    barrier = pltpu.get_barrier_semaphore()
+    for o in range(1, 8):
+        pl.semaphore_signal(barrier, inc=1, device_id=(peer(o), z), device_id_type=MESH)
+    for o in range(1, 4):
+        pl.semaphore_signal(barrier, inc=1, device_id=(d, (z + o) % 4), device_id_type=MESH)
+    pl.semaphore_wait(barrier, 10)
+
+    z_copies = [
+        remote(x_ref, zbuf.at[z], zs.at[o - 1], zr.at[o - 1], d, (z + o) % 4)
+        for o in (2, 1, 3)
+    ]
+    t_copies = [
+        remote(tscr, tabs.at[d], ts.at[o - 1], tr.at[o - 1], peer(o), z) for o in range(1, 8)
+    ]
+    for copy in z_copies + t_copies:
+        copy.start()
+    zbuf[pl.ds(z, 1)] = x_ref[...][None]
+    tabs[pl.ds(d, 1)] = tscr[...][None]
+
+    ro = lax.broadcasted_iota(jnp.int32, (cap, rows), 0)
+    rj = lax.broadcasted_iota(jnp.int32, (cap, rows), 1)
+    for p in range(n_dp):
+        start = tscr[0:1, p:p + 1]
+        length = tscr[1:2, p:p + 1]
+        pick = jnp.where((rj - ro == start) & (ro < length), 1.0, 0.0).astype(BF)
+        outr[p] = jnp.dot(pick, x_ref[...], preferred_element_type=F32).astype(BF)
+    r_copies = [
+        remote(outr.at[peer(o)], arr.at[d], rs.at[o - 1], rr.at[o - 1], peer(o), z)
+        for o in (6, 7, 2, 3, 4, 5, 1)
+    ]
+    for copy in r_copies:
+        copy.start()
+    arr[pl.ds(d, 1)] = outr[pl.ds(d, 1)]
+
+    for copy in t_copies:
+        copy.wait_recv()
+    pi = lax.broadcasted_iota(jnp.int32, (rows, rows), 0)
+    pj = lax.broadcasted_iota(jnp.int32, (rows, rows), 1)
+    delta = pi - pj
+    for p in range(n_dp):
+        spot = pl.multiple_of((p // 2 + 4 * (1 - (p % 2 + k) % 2)) * rows, rows)
+        for s in range(n_dp):
+            start = tabs[s, 0:1, p:p + 1]
+            length = tabs[s, 1:2, p:p + 1]
+            slot = tabs[p, 2:3, s:s + 1]
+            hit = (delta == slot - start) & (pj >= start) & (pj < start + length)
+            perm[pl.ds(spot, rows), s * rows:(s + 1) * rows] = jnp.where(hit, 1.0, 0.0).astype(BF)
+
+    for copy in z_copies:
+        copy.wait_recv()
+
+    step = 16
+    total = float(feat * 4)
+
+    def norm_rows(i, carry):
+        span = pl.ds(pl.multiple_of(i * step, step), step)
+        s1 = jnp.zeros((step, 1), F32)
+        s2 = jnp.zeros((step, 1), F32)
+        for b in range(4):
+            v = zbuf[b, span, :].astype(F32)
+            s1 += jnp.sum(v, axis=-1, keepdims=True)
+            s2 += jnp.sum(v * v, axis=-1, keepdims=True)
+        mid = s1 / total
+        scale = lax.rsqrt(s2 / total - mid * mid + epsilon)
+        for b in range(n_dp):
+            lane = (b % 2) * kdim
+            v = zbuf[b // 2, span, lane:lane + kdim].astype(F32)
+            g = ng_ref[:, b * kdim:(b + 1) * kdim]
+            nbuf[b, span, :] = ((v - mid) * scale * g).astype(BF)
+        return carry
+
+    lax.fori_loop(0, rows // step, norm_rows, 0)
+
+    a_copies = [
+        remote(nbuf.at[peer(o)], gbuf.at[d], asem.at[o - 1], ar.at[o - 1], peer(o), z)
+        for o in (6, 7, 2, 3, 4, 5, 1)
+    ]
+    for copy in a_copies:
+        copy.start()
+    gbuf[pl.ds(d, 1)] = nbuf[pl.ds(d, 1)]
+
+    for copy in r_copies:
+        copy.wait_recv()
+    si = lax.broadcasted_iota(jnp.int32, (rows, cap), 0)
+    so = lax.broadcasted_iota(jnp.int32, (rows, cap), 1)
+    place = jnp.concatenate(
+        [
+            jnp.where(si - so == tscr[2:3, s:s + 1], 1.0, 0.0)
+            for s in range(n_dp)
+        ],
+        axis=1,
+    ).astype(BF)
+    packed_ref[...] = jnp.dot(
+        place, arr[...].reshape(n_dp * cap, feat), preferred_element_type=F32
+    ).astype(BF)
+
+    for copy in a_copies:
+        copy.wait_recv()
+    w_copy.wait()
+
+    tile = 256
+
+    def order_half(h):
+        def body(t, carry):
+            lane = pl.ds(pl.multiple_of(t * tile, tile), tile)
+            right = gbuf[:, :, lane].reshape(n_dp * rows, tile)
+            ordr[:, lane] = jnp.dot(
+                perm[h * half:(h + 1) * half, :], right, preferred_element_type=F32
+            ).astype(BF)
+            return carry
+
+        lax.fori_loop(0, kdim // tile, body, 0)
+
+    order_half(0)
+    sibling = peer(1)
+    s_copies = []
+    for j in range(3):
+        def body(t, carry, j=j):
+            lane = pl.ds(pl.multiple_of(t * tile, tile), tile)
+            sbuf[j, :, lane] = jnp.dot(
+                ordr[...], w_ref[j, :, lane], preferred_element_type=F32
+            ).astype(BF)
+            return carry
+
+        lax.fori_loop(0, cols // tile, body, 0)
+        copy = remote(sbuf.at[j], rbuf.at[j], ssem.at[j], sr.at[j], sibling, z)
+        copy.start()
+        s_copies.append(copy)
+
+    order_half(1)
+    c_copies = [[], [], []]
+    for j in range(3):
+        s_copies[j].wait_recv()
+
+        def body(t, carry, j=j):
+            lane = pl.ds(pl.multiple_of(t * tile, tile), tile)
+            got = jnp.dot(ordr[...], w_ref[j, :, lane], preferred_element_type=F32)
+            got = (got + rbuf[j, :, lane].astype(F32)).astype(BF)
+            cbuf[j, :, :, lane] = got.reshape(half // rows, rows, tile)
+            return carry
+
+        lax.fori_loop(0, cols // tile, body, 0)
+        for oc in (3, 1, 2):
+            copy = remote(
+                cbuf.at[j, peer_chip(oc)], crecv.at[j, oc - 1],
+                cs.at[j, oc - 1], cr.at[j, oc - 1], peer(2 * oc), z,
+            )
+            copy.start()
+            c_copies[j].append(copy)
+
+    hs = qg_ref.shape[1]
+    heads = cols // hs
+    chip = d // 2
+
+    for j in range(3):
+        for copy in c_copies[j]:
+            copy.wait_recv()
+        for h in range(heads):
+            lane = slice(h * hs, (h + 1) * hs)
+            v = cbuf[j, pl.ds(chip, 1), :, lane][0].astype(F32)
+            for b in range(3):
+                v += crecv[j, b, :, lane].astype(F32)
+            if j < 2:
+                mid = jnp.mean(v, axis=-1, keepdims=True)
+                spread = jnp.mean(v * v, axis=-1, keepdims=True) - mid * mid
+                gain = (qg_ref, kg_ref)[j][...]
+                v = (v - mid) * lax.rsqrt(spread + epsilon) * gain
+            (qn, kn, vn)[j][:, lane] = v.astype(BF)
+
+    ids = jnp.broadcast_to(ids_ref[...], (rows, rows))
+    same = ids == ids.T
+    for h in range(heads):
+        lane = slice(h * hs, (h + 1) * hs)
+        scores = lax.dot_general(
+            qn[:, lane], kn[:, lane], (((1,), (1,)), ((), ())), preferred_element_type=F32
+        ) * hs ** (-0.5)
+        raw = jnp.where(same, jnp.exp(scores), 0.0)
+        att = (raw / jnp.sum(raw, axis=-1, keepdims=True)).astype(BF)
+        ctx[:, lane] = jnp.dot(att, vn[:, lane], preferred_element_type=F32).astype(BF)
+
+    ow_copy.wait()
+    wide = 512
+    p_copies = []
+    for i, o in enumerate((2, 1, 3, 0)):
+        goal = (z + o) % 4
+
+        def body(t, carry, i=i, goal=goal):
+            lane = pl.ds(pl.multiple_of(t * wide, wide), wide)
+            from_lane = pl.ds(pl.multiple_of(goal * feat + t * wide, wide), wide)
+            pbuf[i, :, lane] = jnp.dot(
+                ctx[...], ow_ref[:, from_lane], preferred_element_type=F32
+            ).astype(BF)
+            return carry
+
+        lax.fori_loop(0, feat // wide, body, 0)
+        if o:
+            copy = remote(pbuf.at[i], zrecv.at[i], ps.at[i], pr.at[i], d, goal)
+            copy.start()
+            p_copies.append(copy)
+    for copy in p_copies:
+        copy.wait_recv()
+    result = pbuf[3].astype(F32)
+    for i in range(3):
+        result += zrecv[i].astype(F32)
+    out_ref[...] = result.astype(BF)
+
+    for copy in z_copies + t_copies + r_copies + a_copies + s_copies + sum(c_copies, []) + p_copies:
+        copy.wait_send()
+
+
+def fused_on_device(
+    patches,
+    send_start,
+    run_length,
+    slot_start,
+    image_ids,
+    norm_gain,
+    qkv_weight,
+    query_gain,
+    key_gain,
+    out_weight,
+):
+    rows, feat = patches.shape
+    n_dp = lax.axis_size("dp")
+    n_mp = lax.axis_size("mp")
+    cap = 2 * rows // n_dp
+    kdim, _, cols = qkv_weight.shape
+    width = out_weight.shape[1]
+    half = n_dp // 2 * rows
+    weight = jnp.transpose(qkv_weight, (1, 0, 2))
+    vm = pl.BlockSpec(memory_space=pltpu.VMEM)
+    hbm = pl.BlockSpec(memory_space=pl.ANY)
+    dma = pltpu.SemaphoreType.DMA
+    return pl.pallas_call(
+        fused_kernel,
+        out_shape=(
+            jax.ShapeDtypeStruct((rows, feat), BF),
+            jax.ShapeDtypeStruct((rows, feat), BF),
+        ),
+        in_specs=[vm] * 8 + [hbm] * 2,
+        out_specs=(vm, vm),
+        scratch_shapes=[
+            pltpu.VMEM((3, kdim, cols), BF),
+            pltpu.VMEM((cols, width), BF),
+            pltpu.VMEM((n_mp, rows, feat), BF),
+            pltpu.VMEM((n_dp, rows, kdim), BF),
+            pltpu.VMEM((n_dp, rows, kdim), BF),
+            pltpu.VMEM((n_dp, cap, feat), BF),
+            pltpu.VMEM((n_dp, cap, feat), BF),
+            pltpu.VMEM((8, 128), jnp.int32),
+            pltpu.VMEM((n_dp, 8, 128), jnp.int32),
+            pltpu.VMEM((2 * half, 2 * half), BF),
+            pltpu.VMEM((half, kdim), BF),
+            pltpu.VMEM((3, half, cols), BF),
+            pltpu.VMEM((3, half, cols), BF),
+            pltpu.VMEM((3, n_dp // 2, rows, cols), BF),
+            pltpu.VMEM((3, n_dp // 2 - 1, rows, cols), BF),
+            pltpu.VMEM((rows, cols), BF),
+            pltpu.VMEM((rows, cols), BF),
+            pltpu.VMEM((rows, cols), BF),
+            pltpu.VMEM((rows, cols), BF),
+            pltpu.VMEM((n_mp, rows, feat), BF),
+            pltpu.VMEM((n_mp - 1, rows, feat), BF),
+            dma((2,)),
+            dma((3,)), dma((3,)),
+            dma((7,)), dma((7,)),
+            dma((7,)), dma((7,)),
+            dma((7,)), dma((7,)),
+            dma((3,)), dma((3,)),
+            dma((3, 3)), dma((3, 3)),
+            dma((3,)), dma((3,)),
+        ],
+        compiler_params=pltpu.CompilerParams(
+            collective_id=0, has_side_effects=True, vmem_limit_bytes=60 * 1024 * 1024
+        ),
+    )(
+        patches, send_start, run_length, slot_start, image_ids,
+        norm_gain.reshape(1, -1), query_gain.reshape(1, -1), key_gain.reshape(1, -1),
+        weight, out_weight,
+    )
+
+
 def solution(mesh):
+    small = mesh.shape["dp"] == 8 and mesh.shape["mp"] == 4
     return jax.shard_map(
-        on_device,
+        fused_on_device if small else plain_on_device,
         mesh=mesh,
         in_specs=(
             P("dp", "mp"),

time: 221 us -> 144 us (0.65)
  Pallas kernels: 0 us -> 139 us
  waiting for transfers between devices: 123 us -> 0 us
  blocking collectives: 37.5 us -> 0 us
  matrix products: 23.2 us -> 0 us
  between operations: 13.9 us -> 0.64 us
  local copies, waits for them, and re-layouts: 12.6 us -> 3.53 us
  starting transfers between devices: 7.45 us -> 0 us
  other arithmetic: 2.56 us -> 0 us
    pallas_call x0 -> x1, Pallas kernels: none -> 139 us  [fused_on_device(): pl.pallas_call(fused_kernel, out_shape=(jax.ShapeDtypeStruct((rows, feat)...]
    reduce_scatter x2 -> x0, waiting for transfers between devices: 75.2 us -> none  [the longest x1 59.1 us: on_device(): lax.psum_scatter(partial, 'dp', scatter_dimension=0, tiled=True)]
    all_gather x1 -> x0, waiting for transfers between devices: 35.5 us -> none  [on_device(): wide = lax.all_gather(normed, 'mp', axis=1, tiled=True)]
    all_gather x1 -> x0, blocking collectives: 24 us -> none  [on_device(): tables = lax.all_gather(tables, 'dp', axis=0, tiled=True)]
    dot_general x6 -> x0, matrix products: 23.2 us -> none  [the longest x1 12.2 us: on_device(): jnp.dot(ordered, qkv_weight.reshape(qkv_weight.shape[0], local_cols), pre...]
    psum x1 -> x0, blocking collectives: 13.5 us -> none  [on_device(): sums = lax.psum(sums, 'mp') / (feat_local * mp_count)]
    all_to_all x2 -> x0, waiting for transfers between devices: 12.4 us -> none  [the longest x1 12.4 us: on_device(): lax.all_to_all(outgoing.reshape(pack_count, capacity, feat_local), 'dp',...]
    all_to_all x2 -> x0, starting transfers between devices: 7.33 us -> none  [the longest x1 3.79 us: on_device(): slices = lax.all_to_all(wide, 'dp', split_axis=1, concat_axis=0, tiled=True)]
  transfers between devices with their start and end apart: 5 -> 0, of which waited for: 4 -> 0; matrix products, arithmetic and copies ran while one was open for 4% -> 0% of each run, Pallas kernels for 0% -> 0%
where the time goes in v2:
time: 144 us; the launch traced here: 143 us
  Pallas kernels  139 us (97%)
  local copies, waits for them, and re-layouts  3.53 us (2%)
    pallas_call x1, Pallas kernels, fused_on_device(): pl.pallas_call(fused_kernel, out_shape=(jax.ShapeDtypeStruct((rows, feat)...  139 us
    unnamed x2, local copies, waits for them, and re-layouts  3.53 us

profile of v2, /device:TPU:0, one launch (start us, length us, event | category | flops | bytes accessed | tf_op | source)
XLA Modules:
  0.0 143.3 jit_solution(10506882405639020451)
XLA Ops:
  0.6 139.2 %shard_map.113 = (bf16[128,1536]{1,0:T(8,128)(2,1)}, bf16[128,1536]{1,0:T(8,128)(2,1)}) custom-call(bf16[128,1536]{1,0:T(8,128)(2,1)} %x_ref.1, s32[1,8]{1,0:T(1,128)} %ss_ref.1, s32[1,8]{1,0:T(1,128)} %rl_ref.1, s32[1,8]{1,0:T(1,128)} %sl_ref.1, s32[1,128]{1,0:T(1,128)} %ids_ref.1, f32[1,6144]{1,0:T(1,128)} %bitcast.5, f32[1,128]{1,0:T(1,128)} %bitcast.6, ...), custom_call_target="tpu_custom_call" | custom-call | tf_op jit(solution)/shard_map/pallas_call | solution.py:381
  139.8 1.8 %copy.14 = bf16[128,1536]{1,0:T(8,128)(2,1)} copy(bf16[128,1536]{1,0:T(8,128)(2,1)} %get-tuple-element.4) | data formatting | bytes 786432
  141.6 1.8 %copy.15 = bf16[128,1536]{1,0:T(8,128)(2,1)} copy(bf16[128,1536]{1,0:T(8,128)(2,1)} %get-tuple-element.5) | data formatting | bytes 786432

commit v3 on v2

--- a/solution.py
+++ b/solution.py
@@ -110,7 +110,7 @@
     x_ref, ss_ref, rl_ref, sl_ref, ids_ref, ng_ref, qg_ref, kg_ref, w_hbm, ow_hbm,
     packed_ref, out_ref,
     w_ref, ow_ref, zbuf, nbuf, gbuf, outr, arr, tscr, tabs, perm, ordr,
-    sbuf, rbuf, cbuf, crecv, qn, kn, vn, ctx, pbuf, zrecv,
+    sbuf, rbuf, cbuf, crecv, qn, kn, vn, ctx, pbuf, psend, zrecv,
     w_sem, zs, zr, asem, ar, rs, rr, ts, tr, ssem, sr, cs, cr, ps, pr,
 ):
     rows, feat = x_ref.shape
@@ -148,20 +148,69 @@
     barrier = pltpu.get_barrier_semaphore()
     for o in range(1, 8):
         pl.semaphore_signal(barrier, inc=1, device_id=(peer(o), z), device_id_type=MESH)
-    for o in range(1, 4):
-        pl.semaphore_signal(barrier, inc=1, device_id=(d, (z + o) % 4), device_id_type=MESH)
-    pl.semaphore_wait(barrier, 10)
-
-    z_copies = [
-        remote(x_ref, zbuf.at[z], zs.at[o - 1], zr.at[o - 1], d, (z + o) % 4)
-        for o in (2, 1, 3)
-    ]
+    for way in range(2):
+        @pl.when(z < 3 if way == 0 else z > 0)
+        def _(way=way):
+            pl.semaphore_signal(
+                barrier, inc=1, device_id=(d, z + 1 - 2 * way), device_id_type=MESH
+            )
+    near = jnp.where((z == 0) | (z == 3), 1, 2)
+    pl.semaphore_wait(barrier, 7 + near)
+
+    hrows = rows // 2
+
+    def z_copy(block, h, way):
+        span = slice(h * hrows, (h + 1) * hrows)
+        return remote(
+            zbuf.at[block, span], zbuf.at[block, span],
+            zs.at[way, h, block], zr.at[h, block], d, z + 1 - 2 * way,
+        )
+
+    def z_send(h, way):
+        @pl.when(z < 3 if way == 0 else z > 0)
+        def _():
+            z_copy(z, h, way).start()
+
+    def z_pass(h):
+        for t in range(1, 4):
+            for way in range(2):
+                block = z - t if way == 0 else z + t
+
+                @pl.when(block >= 0 if way == 0 else block <= 3)
+                def _(block=block, way=way):
+                    z_copy(block, h, way).wait_recv()
+
+                    @pl.when(z < 3 if way == 0 else z > 0)
+                    def _():
+                        z_copy(block, h, way).start()
+
+                if h == 0:
+                    @pl.when(z == t if way == 0 else z == 3 - t)
+                    def _(way=way):
+                        z_send(1, way)
+
+    def z_drain():
+        for h in range(2):
+            for t in range(4):
+                for way in range(2):
+                    block = z - t if way == 0 else z + t
+
+                    @pl.when((block >= 0) & (z < 3) if way == 0 else (block <= 3) & (z > 0))
+                    def _(block=block, way=way, h=h):
+                        z_copy(block, h, way).wait_send()
+
+    zbuf[pl.ds(z, 1)] = x_ref[...][None]
+    for way in range(2):
+        z_send(0, way)
+        @pl.when(z == 0 if way == 0 else z == 3)
+        def _(way=way):
+            z_send(1, way)
+
     t_copies = [
         remote(tscr, tabs.at[d], ts.at[o - 1], tr.at[o - 1], peer(o), z) for o in range(1, 8)
     ]
-    for copy in z_copies + t_copies:
+    for copy in t_copies:
         copy.start()
-    zbuf[pl.ds(z, 1)] = x_ref[...][None]
     tabs[pl.ds(d, 1)] = tscr[...][None]
 
     ro = lax.broadcasted_iota(jnp.int32, (cap, rows), 0)
@@ -178,23 +227,6 @@
     for copy in r_copies:
         copy.start()
     arr[pl.ds(d, 1)] = outr[pl.ds(d, 1)]
-
-    for copy in t_copies:
-        copy.wait_recv()
-    pi = lax.broadcasted_iota(jnp.int32, (rows, rows), 0)
-    pj = lax.broadcasted_iota(jnp.int32, (rows, rows), 1)
-    delta = pi - pj
-    for p in range(n_dp):
-        spot = pl.multiple_of((p // 2 + 4 * (1 - (p % 2 + k) % 2)) * rows, rows)
-        for s in range(n_dp):
-            start = tabs[s, 0:1, p:p + 1]
-            length = tabs[s, 1:2, p:p + 1]
-            slot = tabs[p, 2:3, s:s + 1]
-            hit = (delta == slot - start) & (pj >= start) & (pj < start + length)
-            perm[pl.ds(spot, rows), s * rows:(s + 1) * rows] = jnp.where(hit, 1.0, 0.0).astype(BF)
-
-    for copy in z_copies:
-        copy.wait_recv()
 
     step = 16
     total = float(feat * 4)
@@ -216,15 +248,33 @@
             nbuf[b, span, :] = ((v - mid) * scale * g).astype(BF)
         return carry
 
-    lax.fori_loop(0, rows // step, norm_rows, 0)
-
-    a_copies = [
-        remote(nbuf.at[peer(o)], gbuf.at[d], asem.at[o - 1], ar.at[o - 1], peer(o), z)
-        for o in (6, 7, 2, 3, 4, 5, 1)
-    ]
-    for copy in a_copies:
-        copy.start()
+    a_copies = []
+    for h in range(2):
+        span = slice(h * hrows, (h + 1) * hrows)
+        z_pass(h)
+        lax.fori_loop(h * (hrows // step), (h + 1) * (hrows // step), norm_rows, 0)
+        for o in (6, 7, 2, 3, 4, 5, 1):
+            copy = remote(
+                nbuf.at[peer(o), span], gbuf.at[d, span],
+                asem.at[h, o - 1], ar.at[h, o - 1], peer(o), z,
+            )
+            copy.start()
+            a_copies.append(copy)
     gbuf[pl.ds(d, 1)] = nbuf[pl.ds(d, 1)]
+
+    for copy in t_copies:
+        copy.wait_recv()
+    pi = lax.broadcasted_iota(jnp.int32, (rows, rows), 0)
+    pj = lax.broadcasted_iota(jnp.int32, (rows, rows), 1)
+    delta = pi - pj
+    for p in range(n_dp):
+        spot = pl.multiple_of((p // 2 + 4 * (1 - (p % 2 + k) % 2)) * rows, rows)
+        for s in range(n_dp):
+            start = tabs[s, 0:1, p:p + 1]
+            length = tabs[s, 1:2, p:p + 1]
+            slot = tabs[p, 2:3, s:s + 1]
+            hit = (delta == slot - start) & (pj >= start) & (pj < start + length)
+            perm[pl.ds(spot, rows), s * rows:(s + 1) * rows] = jnp.where(hit, 1.0, 0.0).astype(BF)
 
     for copy in r_copies:
         copy.wait_recv()
@@ -248,24 +298,27 @@
     tile = 256
 
     def order_half(h):
+        span = slice(h * half, (h + 1) * half)
+
         def body(t, carry):
             lane = pl.ds(pl.multiple_of(t * tile, tile), tile)
             right = gbuf[:, :, lane].reshape(n_dp * rows, tile)
-            ordr[:, lane] = jnp.dot(
-                perm[h * half:(h + 1) * half, :], right, preferred_element_type=F32
+            ordr[span, lane] = jnp.dot(
+                perm[span, :], right, preferred_element_type=F32
             ).astype(BF)
             return carry
 
         lax.fori_loop(0, kdim // tile, body, 0)
 
-    order_half(0)
     sibling = peer(1)
     s_copies = []
-    for j in range(3):
-        def body(t, carry, j=j):
+    c_copies = [[], [], []]
+
+    def sibling_part(j):
+        def body(t, carry):
             lane = pl.ds(pl.multiple_of(t * tile, tile), tile)
             sbuf[j, :, lane] = jnp.dot(
-                ordr[...], w_ref[j, :, lane], preferred_element_type=F32
+                ordr[:half, :], w_ref[j, :, lane], preferred_element_type=F32
             ).astype(BF)
             return carry
 
@@ -274,14 +327,12 @@
         copy.start()
         s_copies.append(copy)
 
-    order_half(1)
-    c_copies = [[], [], []]
-    for j in range(3):
+    def own_part(j):
         s_copies[j].wait_recv()
 
-        def body(t, carry, j=j):
+        def body(t, carry):
             lane = pl.ds(pl.multiple_of(t * tile, tile), tile)
-            got = jnp.dot(ordr[...], w_ref[j, :, lane], preferred_element_type=F32)
+            got = jnp.dot(ordr[half:, :], w_ref[j, :, lane], preferred_element_type=F32)
             got = (got + rbuf[j, :, lane].astype(F32)).astype(BF)
             cbuf[j, :, :, lane] = got.reshape(half // rows, rows, tile)
             return carry
@@ -294,6 +345,15 @@
             )
             copy.start()
             c_copies[j].append(copy)
+
+    order_half(0)
+    sibling_part(0)
+    order_half(1)
+    sibling_part(1)
+    own_part(0)
+    sibling_part(2)
+    own_part(1)
+    own_part(2)
 
     hs = qg_ref.shape[1]
     heads = cols // hs
@@ -327,32 +387,71 @@
 
     ow_copy.wait()
     wide = 512
-    p_copies = []
-    for i, o in enumerate((2, 1, 3, 0)):
-        goal = (z + o) % 4
-
-        def body(t, carry, i=i, goal=goal):
+
+    def p_copy(m, way):
+        return remote(
+            psend.at[m], zrecv.at[way, m], ps.at[m], pr.at[way, m], d, z + 1 - 2 * way
+        )
+
+    for m in (3, 0, 2, 1):
+        def body(t, carry, m=m):
             lane = pl.ds(pl.multiple_of(t * wide, wide), wide)
-            from_lane = pl.ds(pl.multiple_of(goal * feat + t * wide, wide), wide)
-            pbuf[i, :, lane] = jnp.dot(
-                ctx[...], ow_ref[:, from_lane], preferred_element_type=F32
-            ).astype(BF)
+            from_lane = pl.ds(pl.multiple_of(m * feat + t * wide, wide), wide)
+            got = jnp.dot(ctx[...], ow_ref[:, from_lane], preferred_element_type=F32)
+            pbuf[m, :, lane] = got.astype(BF)
             return carry
 
         lax.fori_loop(0, feat // wide, body, 0)
-        if o:
-            copy = remote(pbuf.at[i], zrecv.at[i], ps.at[i], pr.at[i], d, goal)
-            copy.start()
-            p_copies.append(copy)
-    for copy in p_copies:
-        copy.wait_recv()
-    result = pbuf[3].astype(F32)
-    for i in range(3):
-        result += zrecv[i].astype(F32)
-    out_ref[...] = result.astype(BF)
-
-    for copy in z_copies + t_copies + r_copies + a_copies + s_copies + sum(c_copies, []) + p_copies:
+
+        for way, end in ((0, 0), (1, 3)):
+            if m != end:
+                @pl.when(z == end)
+                def _(m=m, way=way):
+                    psend[m] = pbuf[m]
+                    p_copy(m, way).start()
+
+    for at, m in ((1, 3), (2, 0), (1, 2), (2, 1), (2, 3), (1, 0)):
+        way = 0 if m > at else 1
+
+        @pl.when(z == at)
+        def _(m=m, way=way):
+            p_copy(m, way).wait_recv()
+            psend[m] = (pbuf[m].astype(F32) + zrecv[way, m].astype(F32)).astype(BF)
+            p_copy(m, way).start()
+
+    for way, end in ((0, 0), (1, 3)):
+        @pl.when(z != end)
+        def _(way=way):
+            p_copy(z, way).wait_recv()
+
+    mine = pbuf[pl.ds(z, 1)][0].astype(F32)
+
+    @pl.when(z == 0)
+    def _():
+        out_ref[...] = (mine + zrecv[1, 0].astype(F32)).astype(BF)
+
+    @pl.when(z == 3)
+    def _():
+        out_ref[...] = (mine + zrecv[0, 3].astype(F32)).astype(BF)
+
+    for at in (1, 2):
+        @pl.when(z == at)
+        def _(at=at):
+            both = zrecv[0, at].astype(F32) + zrecv[1, at].astype(F32)
+            out_ref[...] = (mine + both).astype(BF)
+
+    for m in range(4):
+        @pl.when(z < m)
+        def _(m=m):
+            p_copy(m, 0).wait_send()
+
+        @pl.when(z > m)
+        def _(m=m):
+            p_copy(m, 1).wait_send()
+
+    for copy in t_copies + r_copies + a_copies + s_copies + sum(c_copies, []):
         copy.wait_send()
+    z_drain()
 
 
 def fused_on_device(
@@ -397,7 +496,7 @@
             pltpu.VMEM((8, 128), jnp.int32),
             pltpu.VMEM((n_dp, 8, 128), jnp.int32),
             pltpu.VMEM((2 * half, 2 * half), BF),
-            pltpu.VMEM((half, kdim), BF),
+            pltpu.VMEM((2 * half, kdim), BF),
             pltpu.VMEM((3, half, cols), BF),
             pltpu.VMEM((3, half, cols), BF),
             pltpu.VMEM((3, n_dp // 2, rows, cols), BF),
@@ -407,15 +506,16 @@
             pltpu.VMEM((rows, cols), BF),
             pltpu.VMEM((rows, cols), BF),
             pltpu.VMEM((n_mp, rows, feat), BF),
-            pltpu.VMEM((n_mp - 1, rows, feat), BF),
+            pltpu.VMEM((n_mp, rows, feat), BF),
+            pltpu.VMEM((2, n_mp, rows, feat), BF),
             dma((2,)),
-            dma((3,)), dma((3,)),
-            dma((7,)), dma((7,)),
+            dma((2, 2, n_mp)), dma((2, n_mp)),
+            dma((2, 7)), dma((2, 7)),
             dma((7,)), dma((7,)),
             dma((7,)), dma((7,)),
             dma((3,)), dma((3,)),
             dma((3, 3)), dma((3, 3)),
-            dma((3,)), dma((3,)),
+            dma((n_mp,)), dma((2, n_mp)),
         ],
         compiler_params=pltpu.CompilerParams(
             collective_id=0, has_side_effects=True, vmem_limit_bytes=60 * 1024 * 1024

time: 144 us -> 131 us (0.910)
  the two profiles are of different devices: /device:TPU:0 before, /device:TPU:8 now
where the time goes in v3:
time: 131 us; the launch traced here: 130 us
  Pallas kernels  126 us (96%)
  local copies, waits for them, and re-layouts  3.53 us (3%)
    pallas_call x1, Pallas kernels, fused_on_device(): pl.pallas_call(fused_kernel, out_shape=(jax.ShapeDtypeStruct((rows, feat)...  126 us
    unnamed x2, local copies, waits for them, and re-layouts  3.53 us

profile of v3, /device:TPU:8, one launch (start us, length us, event | category | flops | bytes accessed | tf_op | source)
XLA Modules:
  0.0 130.3 jit_solution(10527409119173672699)
XLA Ops:
  0.6 126.2 %shard_map.113 = (bf16[128,1536]{1,0:T(8,128)(2,1)}, bf16[128,1536]{1,0:T(8,128)(2,1)}) custom-call(bf16[128,1536]{1,0:T(8,128)(2,1)} %x_ref.1, s32[1,8]{1,0:T(1,128)} %ss_ref.1, s32[1,8]{1,0:T(1,128)} %rl_ref.1, s32[1,8]{1,0:T(1,128)} %sl_ref.1, s32[1,128]{1,0:T(1,128)} %ids_ref.1, f32[1,6144]{1,0:T(1,128)} %bitcast.5, f32[1,128]{1,0:T(1,128)} %bitcast.6, ...), custom_call_target="tpu_custom_call" | custom-call | tf_op jit(solution)/shard_map/pallas_call | solution.py:480
  126.8 1.8 %copy.14 = bf16[128,1536]{1,0:T(8,128)(2,1)} copy(bf16[128,1536]{1,0:T(8,128)(2,1)} %get-tuple-element.4) | data formatting | bytes 786432
  128.6 1.8 %copy.15 = bf16[128,1536]{1,0:T(8,128)(2,1)} copy(bf16[128,1536]{1,0:T(8,128)(2,1)} %get-tuple-element.5) | data formatting | bytes 786432

commit v4 on v3

--- a/solution.py
+++ b/solution.py
@@ -157,7 +157,8 @@
     near = jnp.where((z == 0) | (z == 3), 1, 2)
     pl.semaphore_wait(barrier, 7 + near)
 
-    hrows = rows // 2
+    pieces = 4
+    hrows = rows // pieces
 
     def z_copy(block, h, way):
         span = slice(h * hrows, (h + 1) * hrows)
@@ -184,13 +185,13 @@
                     def _():
                         z_copy(block, h, way).start()
 
-                if h == 0:
+                if h + 2 < pieces:
                     @pl.when(z == t if way == 0 else z == 3 - t)
                     def _(way=way):
-                        z_send(1, way)
+                        z_send(h + 2, way)
 
     def z_drain():
-        for h in range(2):
+        for h in range(pieces):
             for t in range(4):
                 for way in range(2):
                     block = z - t if way == 0 else z + t
@@ -202,9 +203,13 @@
     zbuf[pl.ds(z, 1)] = x_ref[...][None]
     for way in range(2):
         z_send(0, way)
+    for way in range(2):
+        z_send(1, way)
+
         @pl.when(z == 0 if way == 0 else z == 3)
         def _(way=way):
-            z_send(1, way)
+            for h in range(2, pieces):
+                z_send(h, way)
 
     t_copies = [
         remote(tscr, tabs.at[d], ts.at[o - 1], tr.at[o - 1], peer(o), z) for o in range(1, 8)
@@ -215,11 +220,18 @@
 
     ro = lax.broadcasted_iota(jnp.int32, (cap, rows), 0)
     rj = lax.broadcasted_iota(jnp.int32, (cap, rows), 1)
-    for p in range(n_dp):
-        start = tscr[0:1, p:p + 1]
-        length = tscr[1:2, p:p + 1]
-        pick = jnp.where((rj - ro == start) & (ro < length), 1.0, 0.0).astype(BF)
-        outr[p] = jnp.dot(pick, x_ref[...], preferred_element_type=F32).astype(BF)
+    pick = jnp.concatenate(
+        [
+            jnp.where(
+                (rj - ro == tscr[0:1, p:p + 1]) & (ro < tscr[1:2, p:p + 1]), 1.0, 0.0
+            )
+            for p in range(n_dp)
+        ],
+        axis=0,
+    ).astype(BF)
+    outr[...] = jnp.dot(
+        pick, x_ref[...], preferred_element_type=F32
+    ).astype(BF).reshape(n_dp, cap, feat)
     r_copies = [
         remote(outr.at[peer(o)], arr.at[d], rs.at[o - 1], rr.at[o - 1], peer(o), z)
         for o in (6, 7, 2, 3, 4, 5, 1)
@@ -249,7 +261,7 @@
         return carry
 
     a_copies = []
-    for h in range(2):
+    for h in range(pieces):
         span = slice(h * hrows, (h + 1) * hrows)
         z_pass(h)
         lax.fori_loop(h * (hrows // step), (h + 1) * (hrows // step), norm_rows, 0)
@@ -393,7 +405,9 @@
             psend.at[m], zrecv.at[way, m], ps.at[m], pr.at[way, m], d, z + 1 - 2 * way
         )
 
-    for m in (3, 0, 2, 1):
+    for i in range(4):
+        m = jnp.where(z < 2, 3 - i, i)
+
         def body(t, carry, m=m):
             lane = pl.ds(pl.multiple_of(t * wide, wide), wide)
             from_lane = pl.ds(pl.multiple_of(m * feat + t * wide, wide), wide)
@@ -404,9 +418,9 @@
         lax.fori_loop(0, feat // wide, body, 0)
 
         for way, end in ((0, 0), (1, 3)):
-            if m != end:
+            if i < 3:
                 @pl.when(z == end)
-                def _(m=m, way=way):
+                def _(m=3 - i if end == 0 else i, way=way):
                     psend[m] = pbuf[m]
                     p_copy(m, way).start()
 
@@ -509,8 +523,8 @@
             pltpu.VMEM((n_mp, rows, feat), BF),
             pltpu.VMEM((2, n_mp, rows, feat), BF),
             dma((2,)),
-            dma((2, 2, n_mp)), dma((2, n_mp)),
-            dma((2, 7)), dma((2, 7)),
+            dma((2, 4, n_mp)), dma((4, n_mp)),
+            dma((4, 7)), dma((4, 7)),
             dma((7,)), dma((7,)),
             dma((7,)), dma((7,)),
             dma((3,)), dma((3,)),

time: 131 us -> 122 us (0.931)
  the two profiles are of different devices: /device:TPU:8 before, /device:TPU:0 now
where the time goes in v4:
time: 122 us
  Pallas kernels  118 us (97%)
  local copies, waits for them, and re-layouts  3.53 us (3%)
    pallas_call x1, Pallas kernels, fused_on_device(): pl.pallas_call(fused_kernel, out_shape=(jax.ShapeDtypeStruct((rows, feat)...  118 us
    unnamed x2, local copies, waits for them, and re-layouts  3.53 us

profile of v4, /device:TPU:0, one launch (start us, length us, event | category | flops | bytes accessed | tf_op | source)
XLA Modules:
  0.0 122.2 jit_solution(3646655272091774212)
XLA Ops:
  0.6 118.0 %shard_map.113 = (bf16[128,1536]{1,0:T(8,128)(2,1)}, bf16[128,1536]{1,0:T(8,128)(2,1)}) custom-call(bf16[128,1536]{1,0:T(8,128)(2,1)} %x_ref.1, s32[1,8]{1,0:T(1,128)} %ss_ref.1, s32[1,8]{1,0:T(1,128)} %rl_ref.1, s32[1,8]{1,0:T(1,128)} %sl_ref.1, s32[1,128]{1,0:T(1,128)} %ids_ref.1, f32[1,6144]{1,0:T(1,128)} %bitcast.5, f32[1,128]{1,0:T(1,128)} %bitcast.6, ...), custom_call_target="tpu_custom_call" | custom-call | tf_op jit(solution)/shard_map/pallas_call | solution.py:494
  118.6 1.8 %copy.14 = bf16[128,1536]{1,0:T(8,128)(2,1)} copy(bf16[128,1536]{1,0:T(8,128)(2,1)} %get-tuple-element.4) | data formatting | bytes 786432
  120.4 1.8 %copy.15 = bf16[128,1536]{1,0:T(8,128)(2,1)} copy(bf16[128,1536]{1,0:T(8,128)(2,1)} %get-tuple-element.5) | data formatting | bytes 786432

commit v5 on v4

--- a/solution.py
+++ b/solution.py
@@ -110,8 +110,8 @@
     x_ref, ss_ref, rl_ref, sl_ref, ids_ref, ng_ref, qg_ref, kg_ref, w_hbm, ow_hbm,
     packed_ref, out_ref,
     w_ref, ow_ref, zbuf, nbuf, gbuf, outr, arr, tscr, tabs, perm, ordr,
-    sbuf, rbuf, cbuf, crecv, qn, kn, vn, ctx, pbuf, psend, zrecv,
-    w_sem, zs, zr, asem, ar, rs, rr, ts, tr, ssem, sr, cs, cr, ps, pr,
+    sbuf, rbuf, cbuf, crecv, fbuf, frecv, qn, kn, vn, ctx, pbuf, psend, zrecv,
+    w_sem, zs, zr, asem, ar, rs, rr, ts, tr, ssem, sr, cs, cr, fs, fr, ps, pr,
 ):
     rows, feat = x_ref.shape
     n_dp, cap = outr.shape[0], outr.shape[1]
@@ -325,6 +325,8 @@
     sibling = peer(1)
     s_copies = []
     c_copies = [[], [], []]
+    f_copies = [[], [], []]
+    part = cols // 2
 
     def sibling_part(j):
         def body(t, carry):
@@ -350,13 +352,29 @@
             return carry
 
         lax.fori_loop(0, cols // tile, body, 0)
-        for oc in (3, 1, 2):
+        for slot in (1, 0):
+            for first in (1, 2):
+                goal = peer_chip(3) if slot else peer_chip(first)
+                copy = remote(
+                    cbuf.at[j, goal, :, (first - 1) * part:first * part],
+                    crecv.at[j, first - 1, slot],
+                    cs.at[j, first - 1, slot], cr.at[j, first - 1, slot], peer(2 * first), z,
+                )
+                copy.start()
+                c_copies[j].append(copy)
+
+    def pass_on(j):
+        for first in (1, 2):
+            c_copies[j][first - 1].wait_recv()
+            own = cbuf[j, pl.ds(peer_chip(3 - first), 1), :, (first - 1) * part:first * part][0]
+            both = own.astype(F32) + crecv[j, first - 1, 1].astype(F32)
+            fbuf[j, first - 1] = both.astype(BF)
             copy = remote(
-                cbuf.at[j, peer_chip(oc)], crecv.at[j, oc - 1],
-                cs.at[j, oc - 1], cr.at[j, oc - 1], peer(2 * oc), z,
+                fbuf.at[j, first - 1], frecv.at[j, first - 1],
+                fs.at[j, first - 1], fr.at[j, first - 1], peer(2 * (3 - first)), z,
             )
             copy.start()
-            c_copies[j].append(copy)
+            f_copies[j].append(copy)
 
     order_half(0)
     sibling_part(0)
@@ -365,20 +383,24 @@
     own_part(0)
     sibling_part(2)
     own_part(1)
+    pass_on(0)
     own_part(2)
+    pass_on(1)
+    pass_on(2)
 
     hs = qg_ref.shape[1]
     heads = cols // hs
     chip = d // 2
 
     for j in range(3):
-        for copy in c_copies[j]:
+        for copy in c_copies[j][2:] + f_copies[j]:
             copy.wait_recv()
         for h in range(heads):
             lane = slice(h * hs, (h + 1) * hs)
             v = cbuf[j, pl.ds(chip, 1), :, lane][0].astype(F32)
-            for b in range(3):
-                v += crecv[j, b, :, lane].astype(F32)
+            way = h * hs // part
+            near = slice(h * hs - way * part, (h + 1) * hs - way * part)
+            v += crecv[j, way, 0, :, near].astype(F32) + frecv[j, way, :, near].astype(F32)
             if j < 2:
                 mid = jnp.mean(v, axis=-1, keepdims=True)
                 spread = jnp.mean(v * v, axis=-1, keepdims=True) - mid * mid
@@ -463,7 +485,7 @@
         def _(m=m):
             p_copy(m, 1).wait_send()
 
-    for copy in t_copies + r_copies + a_copies + s_copies + sum(c_copies, []):
+    for copy in t_copies + r_copies + a_copies + s_copies + sum(c_copies + f_copies, []):
         copy.wait_send()
     z_drain()
 
@@ -514,7 +536,9 @@
             pltpu.VMEM((3, half, cols), BF),
             pltpu.VMEM((3, half, cols), BF),
             pltpu.VMEM((3, n_dp // 2, rows, cols), BF),
-            pltpu.VMEM((3, n_dp // 2 - 1, rows, cols), BF),
+            pltpu.VMEM((3, 2, 2, rows, cols // 2), BF),
+            pltpu.VMEM((3, 2, rows, cols // 2), BF),
+            pltpu.VMEM((3, 2, rows, cols // 2), BF),
             pltpu.VMEM((rows, cols), BF),
             pltpu.VMEM((rows, cols), BF),
             pltpu.VMEM((rows, cols), BF),
@@ -528,7 +552,8 @@
             dma((7,)), dma((7,)),
             dma((7,)), dma((7,)),
             dma((3,)), dma((3,)),
-            dma((3, 3)), dma((3, 3)),
+            dma((3, 2, 2)), dma((3, 2, 2)),
+            dma((3, 2)), dma((3, 2)),
             dma((n_mp,)), dma((2, n_mp)),
         ],
         compiler_params=pltpu.CompilerParams(

time: 122 us -> 114 us (0.934)
  Pallas kernels: 118 us -> 110 us
    pallas_call x1, Pallas kernels: 118 us -> 110 us  [fused_on_device(): pl.pallas_call(fused_kernel, out_shape=(jax.ShapeDtypeStruct((rows, feat)...]
where the time goes in v5:
time: 114 us
  Pallas kernels  110 us (96%)
  local copies, waits for them, and re-layouts  3.53 us (3%)
    pallas_call x1, Pallas kernels, fused_on_device(): pl.pallas_call(fused_kernel, out_shape=(jax.ShapeDtypeStruct((rows, feat)...  110 us
    unnamed x2, local copies, waits for them, and re-layouts  3.53 us

profile of v5, /device:TPU:0, one launch (start us, length us, event | category | flops | bytes accessed | tf_op | source)
XLA Modules:
  0.0 113.8 jit_solution(11005194785342971347)
XLA Ops:
  0.6 109.6 %shard_map.113 = (bf16[128,1536]{1,0:T(8,128)(2,1)}, bf16[128,1536]{1,0:T(8,128)(2,1)}) custom-call(bf16[128,1536]{1,0:T(8,128)(2,1)} %x_ref.1, s32[1,8]{1,0:T(1,128)} %ss_ref.1, s32[1,8]{1,0:T(1,128)} %rl_ref.1, s32[1,8]{1,0:T(1,128)} %sl_ref.1, s32[1,128]{1,0:T(1,128)} %ids_ref.1, f32[1,6144]{1,0:T(1,128)} %bitcast.5, f32[1,128]{1,0:T(1,128)} %bitcast.6, ...), custom_call_target="tpu_custom_call" | custom-call | tf_op jit(solution)/shard_map/pallas_call | solution.py:516
  110.2 1.8 %copy.14 = bf16[128,1536]{1,0:T(8,128)(2,1)} copy(bf16[128,1536]{1,0:T(8,128)(2,1)} %get-tuple-element.4) | data formatting | bytes 786432
  112.0 1.8 %copy.15 = bf16[128,1536]{1,0:T(8,128)(2,1)} copy(bf16[128,1536]{1,0:T(8,128)(2,1)} %get-tuple-element.5) | data formatting | bytes 786432
